TPU v7x, 768 devices: a whole 4x8x12 slice. The times are simulated.
768 devices in a mesh: grp: 32 (over x, y), sec: 24 (over z, core).
Axes of the slice: x: 4, y: 8, z: 12, core: 2. Of those that a mesh axis runs over, the one named last changes fastest.
Arguments:
- wavefunction: bfloat16 [512, 96, 512], P('grp', 'sec'), may hold values from -6 to 6
- left_ops: bfloat16 [3072, 512, 512], P(('grp', 'sec')), may hold values from -0.25 to 0.25
- right_ops: bfloat16 [3072, 512, 512], P(('grp', 'sec')), may hold values from -0.046875 to 0.046875
- in_sector: int32 [3072], P(('grp', 'sec')), may hold values from 0 to 3
- out_sector: int32 [3072], P(('grp', 'sec')), may hold values from 0 to 3
- term_count: int32 [768], P(('grp', 'sec')), may hold values from 1 to 4
Outputs:
- sigma_block: bfloat16 [512, 96, 512], P('grp', 'sec')
Inputs may be any that keep to these rules, and one draw needn't show every extreme that they name: `term_count`: each device has between 1 and 4 live slots; its live slots come first.
All inputs are finite; a program needn't handle non-finite values.
Results may differ from a plain program's by a relative error of at most 0.0049.
Values may be sent and summed in bfloat16 or wider, within the bound.
A program may use at most 32 MiB of HBM per device.

v0:
```python
import jax
import jax.numpy as jnp
from jax import lax
from jax.sharding import PartitionSpec as P


def on_device(wavefunction, left_ops, right_ops, in_sector, out_sector, term_count):
    slot_count = left_ops.shape[0]
    block_order = left_ops.shape[1]
    sectors = wavefunction.shape[1]
    own_count = term_count[0]
    full_state = lax.all_gather(wavefunction, "grp", axis=0, tiled=True)

    def pick(index):
        left_block = lax.dynamic_index_in_dim(left_ops, index, 0, keepdims=False)
        right_block = lax.dynamic_index_in_dim(right_ops, index, 0, keepdims=False)
        return (left_block, right_block, in_sector[index], out_sector[index])

    def left_step(index, stored):
        left_block, right_block, source, target = pick(index)
        chosen = lax.dynamic_index_in_dim(full_state, source, 1, keepdims=False)
        product = jnp.dot(left_block, chosen, preferred_element_type=jnp.float32).astype(
            jnp.bfloat16
        )
        return lax.dynamic_update_index_in_dim(stored, product, index, 0)

    left_state = lax.fori_loop(
        0, own_count, left_step, jnp.zeros((slot_count, block_order, block_order), jnp.bfloat16)
    )

    def right_step(index, running):
        left_block, right_block, source, target = pick(index)
        product = lax.dynamic_index_in_dim(left_state, index, 0, keepdims=False)
        projected = jnp.einsum(
            "kc,dc->kd", product, right_block, preferred_element_type=jnp.float32
        )
        current = lax.dynamic_index_in_dim(running, target, 1, keepdims=False)
        return lax.dynamic_update_index_in_dim(running, current + projected, target, 1)

    start_sum = jnp.zeros((block_order, sectors, block_order), jnp.float32)
    summed = lax.psum_scatter(
        lax.fori_loop(0, own_count, right_step, start_sum), "grp", scatter_dimension=0, tiled=True
    )
    return summed.astype(jnp.bfloat16)


def solution(mesh):
    return jax.shard_map(
        on_device,
        mesh=mesh,
        in_specs=(
            P("grp", "sec", None),
            P(("grp", "sec"), None, None),
            P(("grp", "sec"), None, None),
            P(("grp", "sec")),
            P(("grp", "sec")),
            P(("grp", "sec")),
        ),
        out_specs=P("grp", "sec", None),
        check_vma=False,
    )
```

profile of v0, /device:TPU:256, one launch (start us, length us, event | category | flops | bytes accessed | tf_op | source)
XLA Modules:
  0.0 425.8 jit_solution(16562526122491389278)
XLA Ops:
  6.5 0.0 copy-start
  6.5 0.0 all-gather.2.cloned.1.call-start
  6.5 1.5 copy.10
  8.0 0.0 all-gather.2.cloned.1.call-update
  8.1 1.3 dynamic-slice
  9.9 93.9 %all-gather.2.cloned.1.call-done = bf16[512,4,512]{2,0,1:T(8,128)(2,1)} async-done(((bf16[16,4,512]{2,0,1:T(8,128)(2,1)}), bf16[512,4,512]{2,0,1:T(8,128)(2,1)}) %all-gather.2.cloned.1.call-update) | async-done | bytes 2097168 | tf_op jit(solution)/shard_map/all_gather | solution.py:12
  103.8 0.2 broadcast_in_dim.17
  103.9 0.0 copy-done
  103.9 20.0 %while.22 = (s32[]{:T(128)}, bf16[4,512,512]{2,1,0:T(8,128)(2,1)S(1)}, s32[]{:T(128)}, bf16[4,512,512]{2,1,0:T(8,128)(2,1)}, s32[4]{0:T(128)S(1)}, /*index=5*/bf...) while((s32[]{:T(128)}, bf16[4,512,512]{2,1,0:T(8,128)(2,1)S(1)}, s32[]{:T(128)}, ...), condition=%wide.region_1.2_spmd, body=%wide.region_0.1_spmd.sunk | while | flops 268697600 | bytes 1574573 | solution.py:27
  104.6 0.6 dynamic_slice.57
  107.1 1.6 fusion.21
  109.4 0.6 dynamic_slice.57
  112.0 1.6 fusion.21
  114.3 0.6 dynamic_slice.57
  116.8 1.6 fusion.21
  119.1 0.6 dynamic_slice.57
  121.7 1.6 fusion.21
  124.0 0.0 copy-start.1
  124.0 2.5 broadcast_in_dim.16.clone
  126.5 0.0 copy-done.1
  126.5 119.9 %while.23 = (s32[]{:T(128)}, f32[512,4,512]{2,1,0:T(4,128)}, s32[]{:T(128)}, s32[4]{0:T(128)S(1)}, bf16[4,512,512]{2,1,0:T(8,128)(2,1)S(1)}, /*index=5*/bf16[4,5...) while((s32[]{:T(128)}, f32[512,4,512]{2,1,0:T(4,128)}, s32[]{:T(128)}, s32[4]{0:T(128)S(1)}, ...), condition=%wide.region_3.4_spmd, body=%wide.region_2.3_spmd.sunk | while | flops 268697600 | bytes 9438389 | solution.py:42
  127.1 0.6 dynamic_slice.61
  129.7 3.1 constant_dynamic-slice_fusion.2
  132.8 1.5 fusion.24
  134.3 1.1 copy.21
  135.4 20.9 %dynamic_update_slice.14 = f32[512,4,512]{2,1,0:T(4,128)} dynamic-update-slice(f32[512,4,512]{2,1,0:T(4,128)} %get-tuple-element.246, f32[512,1,512]{2,1,0:T(1,128)S(1)} %copy.21, s32[]{:T(128)} %constant.45.clone.1..sunk.1, s32[]{:T(128)S(6)} %select_n.33, s32[]{:T(128)} %constant.45.clone.1..sunk.1) | dynamic-update-slice | bytes 2097156 | tf_op jit(solution)/shard_map/while/body/jit(dynamic_update_index_in_dim)/dynamic_update_slice | solution.py:38
  156.9 0.6 dynamic_slice.61
  159.5 3.1 constant_dynamic-slice_fusion.2
  162.6 1.5 fusion.24
  164.1 1.1 copy.21
  165.2 20.9 %dynamic_update_slice.14 = f32[512,4,512]{2,1,0:T(4,128)} dynamic-update-slice(f32[512,4,512]{2,1,0:T(4,128)} %get-tuple-element.246, f32[512,1,512]{2,1,0:T(1,128)S(1)} %copy.21, s32[]{:T(128)} %constant.45.clone.1..sunk.1, s32[]{:T(128)S(6)} %select_n.33, s32[]{:T(128)} %constant.45.clone.1..sunk.1) | dynamic-update-slice | bytes 2097156 | tf_op jit(solution)/shard_map/while/body/jit(dynamic_update_index_in_dim)/dynamic_update_slice | solution.py:38
  186.8 0.6 dynamic_slice.61
  189.3 3.1 constant_dynamic-slice_fusion.2
  192.4 1.5 fusion.24
  193.9 1.1 copy.21
  195.0 20.9 %dynamic_update_slice.14 = f32[512,4,512]{2,1,0:T(4,128)} dynamic-update-slice(f32[512,4,512]{2,1,0:T(4,128)} %get-tuple-element.246, f32[512,1,512]{2,1,0:T(1,128)S(1)} %copy.21, s32[]{:T(128)} %constant.45.clone.1..sunk.1, s32[]{:T(128)S(6)} %select_n.33, s32[]{:T(128)} %constant.45.clone.1..sunk.1) | dynamic-update-slice | bytes 2097156 | tf_op jit(solution)/shard_map/while/body/jit(dynamic_update_index_in_dim)/dynamic_update_slice | solution.py:38
  216.6 0.6 dynamic_slice.61
  219.1 3.1 constant_dynamic-slice_fusion.2
  222.2 1.5 fusion.24
  223.7 1.1 copy.21
  224.8 20.9 %dynamic_update_slice.14 = f32[512,4,512]{2,1,0:T(4,128)} dynamic-update-slice(f32[512,4,512]{2,1,0:T(4,128)} %get-tuple-element.246, f32[512,1,512]{2,1,0:T(1,128)S(1)} %copy.21, s32[]{:T(128)} %constant.45.clone.1..sunk.1, s32[]{:T(128)S(6)} %select_n.33, s32[]{:T(128)} %constant.45.clone.1..sunk.1) | dynamic-update-slice | bytes 2097156 | tf_op jit(solution)/shard_map/while/body/jit(dynamic_update_index_in_dim)/dynamic_update_slice | solution.py:38
  246.4 171.9 %all-reduce.2 = bf16[512,4,512]{2,1,0:T(4,128)(2,1)S(1)} all-reduce(f32[512,4,512]{2,1,0:T(4,128)} %get-tuple-element.108), channel_id=2, replica_groups=mesh['grp'=32,'sec'=24] {'grp'}, use_global_device_ids=true, to_apply=%region_4.5.clone | all-reduce | flops 1048576 | bytes 6291456
  418.3 0.7 dynamic-slice_convert_fusion
Async XLA Ops:
  6.5 97.4 %copy-start = (s32[4]{0:T(128)S(1)}, s32[4]{0:T(128)}, u32[]{:S(2)}) copy-start(s32[4]{0:T(128)} %param.13) | copy-start | bytes 52
  6.5 97.2 %all-gather.2.cloned.1.call-start = ((), (), s32[]{:S(2)}) async-start(), calls=%async_computation | async-start | bytes 2162688 | tf_op jit(solution)/shard_map/all_gather | solution.py:12
  124.0 2.5 copy-start.1
Sparse Core Ops, SparseCore 0:
  11.1 92.5 all-gather.1
where the time goes:
time: 429 us; the launch traced here: 426 us
  blocking collectives  172 us (40%)
  local copies, waits for them, and re-layouts  111 us (26%)
  waiting for transfers between devices  93.9 us (22%)
  loops' own time  22.3 us (5%)
  between operations  14 us (3%)
  matrix products  12.6 us (3%)
    unnamed x1, blocking collectives  172 us
    all_gather x1, waiting for transfers between devices, on_device(): full_state = lax.all_gather(wavefunction, 'grp', axis=0, tiled=True)  93.9 us
    dynamic_update_slice x8, local copies, waits for them, and re-layouts, right_step(): lax.dynamic_update_index_in_dim(running, current + projected, target, 1)  88 us
    dynamic_slice x4, local copies, waits for them, and re-layouts, right_step(): current = lax.dynamic_index_in_dim(running, target, 1, keepdims=False)  12.4 us
    another operation x1, loops' own time, on_device(): lax.fori_loop(0, own_count, right_step, start_sum)  11.2 us
    another operation x1, loops' own time, on_device(): lax.fori_loop(0, own_count, left_step, jnp.zeros((slot_count, block_order...  11.1 us
  transfers between devices with their start and end apart: 1, of which 1 were waited for; matrix products, arithmetic and copies ran while one was open for 0% of the time, Pallas kernels for 0%

commit v1 on v0

v1 whole, which is shorter than its diff:
```python
import jax
import jax.numpy as jnp
from jax import lax
from jax.experimental import pallas as pl
from jax.experimental.pallas import tpu as pltpu
from jax.sharding import PartitionSpec as P

NX, NY = 4, 8
MESH = pl.DeviceIdType.MESH


def kernel(
    in_ref, out_ref, count_ref, own_ref, left_hbm, right_hbm, o_ref,
    state, left, right, prod, part, fbuf,
    y_send, y_recv, x_send, x_recv,
    load_sem, agx_ss, agx_rs, agy_ss, agy_rs, rsy_ss, rsy_rs, rsx_ss, rsx_rs,
):
    g = lax.axis_index("grp")
    x, y = g // NY, lax.rem(g, NY)
    half = o_ref.shape[2] // 2

    def dev(dx, dy):
        return {"grp": lax.rem(x + dx + NX, NX) * NY + lax.rem(y + dy + NY, NY)}

    loads = [
        pltpu.make_async_copy(left_hbm, left, load_sem.at[0]),
        pltpu.make_async_copy(right_hbm, right, load_sem.at[1]),
        pltpu.make_async_copy(own_ref, state.at[x, y], load_sem.at[2]),
    ]
    for load in loads:
        load.start()

    barrier = pltpu.get_barrier_semaphore()
    peers = [(1, 0), (2, 0), (3, 0), (0, 1), (0, -1)]
    for dx, dy in peers:
        pl.semaphore_signal(barrier, inc=1, device_id=dev(dx, dy), device_id_type=MESH)
    pl.semaphore_wait(barrier, len(peers))

    started = []

    def remote(src, dst, ss, rs, where):
        copy = pltpu.make_async_remote_copy(
            src_ref=src, dst_ref=dst, send_sem=ss, recv_sem=rs, device_id=where, device_id_type=MESH
        )
        copy.start()
        started.append(copy)
        return copy

    gx = [
        remote(own_ref, state.at[x, y], agx_ss.at[j - 1], agx_rs.at[j - 1], dev(j, 0))
        for j in (1, 3, 2)
    ]
    loads[2].wait()
    for copy in gx:
        copy.wait_recv()

    def ring(k, h, d):
        block = lax.rem(y - d * (k - 1) + NY, NY)
        piece = state.at[2 * h:2 * h + 2, block]
        i = (1 - d) // 2
        return remote(piece, piece, agy_ss.at[i, k - 1, h], agy_rs.at[i, k - 1, h], dev(0, d))

    held = {}
    for k in range(1, 5):
        for h in range(2):
            for d in (1, -1):
                if k > 1:
                    held[k - 1, h, d].wait_recv()
                if k < 4 or (h == 0) == (d == 1):
                    held[k, h, d] = ring(k, h, d)
    held[4, 0, 1].wait_recv()
    held[4, 1, -1].wait_recv()

    loads[0].wait()
    rows = NX * NY * own_ref.shape[1]

    def first(q, carry):
        block = state[:, :, in_ref[q]].reshape(rows, 2 * half)
        for m in range(2):
            span = slice(m * (rows // 2), (m + 1) * (rows // 2))
            prod[q, span] = jnp.dot(
                left[q, span], block, preferred_element_type=jnp.float32
            ).astype(jnp.bfloat16)
        return carry

    lax.fori_loop(0, 4, first, 0)
    loads[1].wait()

    weight = [
        [
            jnp.where((out_ref[q] == t) & (q < count_ref[0]), jnp.float32(1), jnp.float32(0))
            for t in range(4)
        ]
        for q in range(4)
    ]

    def second(c, h):
        span = slice(h * (rows // 2), (h + 1) * (rows // 2))
        proj = [
            lax.dot_general(
                prod[q, span], right[q, c * half:(c + 1) * half],
                (((1,), (1,)), ((), ())), preferred_element_type=jnp.float32,
            )
            for q in range(4)
        ]
        for t in range(4):
            total = proj[0] * weight[0][t]
            for q in range(1, 4):
                total = total + proj[q] * weight[q][t]
            part[c, 2 * h:2 * h + 2, :, t] = total.reshape(2, NY, own_ref.shape[1], half)

    def scatter(c):
        got = {}

        def step(k, h, d):
            i = (1 - d) // 2
            value = part[c, 2 * h:2 * h + 2, lax.rem(y + d * k + NY, NY)]
            if (k + 1, h, d) in got:
                got[k + 1, h, d].wait_recv()
                value = value + y_recv[c, i, k, h].astype(jnp.float32)
            y_send[c, i, k - 1, h] = value.astype(jnp.bfloat16)
            got[k, h, d] = remote(
                y_send.at[c, i, k - 1, h], y_recv.at[c, i, k - 1, h],
                rsy_ss.at[c, i, k - 1, h], rsy_rs.at[c, i, k - 1, h], dev(0, d),
            )

        step(4, 0, 1), step(4, 1, -1), step(3, 1, 1), step(3, 0, -1)
        yield
        step(3, 0, 1), step(3, 1, -1)
        yield
        for k in (2, 1):
            step(k, 1, 1), step(k, 0, -1)
            yield
            step(k, 0, 1), step(k, 1, -1)
            yield
        for h in (0, 1):
            value = part[c, 2 * h:2 * h + 2, y]
            for d in (1, -1):
                got[1, h, d].wait_recv()
                value = value + y_recv[c, (1 - d) // 2, 0, h].astype(jnp.float32)
            fbuf[c, 2 * h:2 * h + 2] = value
        cross = []
        for j in (2, 1, 3):
            x_send[c, j - 1] = fbuf[c, lax.rem(x + j, NX)].astype(jnp.bfloat16)
            cross.append(remote(
                x_send.at[c, j - 1], x_recv.at[c, j - 1],
                rsx_ss.at[c, j - 1], rsx_rs.at[c, j - 1], dev(j, 0),
            ))
        yield
        value = fbuf[c, x]
        for copy in cross:
            copy.wait_recv()
        for j in (1, 2, 3):
            value = value + x_recv[c, j - 1].astype(jnp.float32)
        o_ref[:, :, c * half:(c + 1) * half] = value.astype(jnp.bfloat16)

    second(0, 0)
    second(0, 1)
    flow0, flow1 = scatter(0), scatter(1)
    next(flow0)
    second(1, 0)
    next(flow0)
    second(1, 1)
    next(flow1)
    live = [flow0, flow1]
    while live:
        for flow in list(live):
            try:
                next(flow)
            except StopIteration:
                live.remove(flow)
    for copy in started:
        copy.wait_send()


def on_device(wavefunction, left_ops, right_ops, in_sector, out_sector, term_count):
    own = wavefunction.transpose(1, 0, 2)
    sectors, block, order = own.shape
    half = order // 2
    slots = left_ops.shape[0]
    vmem = pl.BlockSpec(memory_space=pltpu.VMEM)
    smem = pl.BlockSpec(memory_space=pltpu.SMEM)
    hbm = pl.BlockSpec(memory_space=pl.ANY)
    dma = pltpu.SemaphoreType.DMA
    result = pl.pallas_call(
        kernel,
        out_shape=jax.ShapeDtypeStruct((sectors, block, order), jnp.bfloat16),
        in_specs=[smem, smem, smem, vmem, hbm, hbm],
        out_specs=vmem,
        scratch_shapes=[
            pltpu.VMEM((NX, NY, sectors, block, order), jnp.bfloat16),
            pltpu.VMEM(left_ops.shape, jnp.bfloat16),
            pltpu.VMEM(right_ops.shape, jnp.bfloat16),
            pltpu.VMEM((slots, left_ops.shape[1], order), jnp.bfloat16),
            pltpu.VMEM((2, NX, NY, sectors, block, half), jnp.float32),
            pltpu.VMEM((2, NX, sectors, block, half), jnp.float32),
            pltpu.VMEM((2, 2, 4, 2, 2, sectors, block, half), jnp.bfloat16),
            pltpu.VMEM((2, 2, 4, 2, 2, sectors, block, half), jnp.bfloat16),
            pltpu.VMEM((2, 3, sectors, block, half), jnp.bfloat16),
            pltpu.VMEM((2, 3, sectors, block, half), jnp.bfloat16),
            dma((3,)),
            dma((3,)), dma((3,)),
            dma((2, 4, 2)), dma((2, 4, 2)),
            dma((2, 2, 4, 2)), dma((2, 2, 4, 2)),
            dma((2, 3)), dma((2, 3)),
        ],
        compiler_params=pltpu.CompilerParams(collective_id=0, has_side_effects=True),
        name="gather_apply_scatter",
    )(in_sector, out_sector, term_count, own, left_ops, right_ops)
    return result.transpose(1, 0, 2)


def solution(mesh):
    return jax.shard_map(
        on_device,
        mesh=mesh,
        in_specs=(
            P("grp", "sec", None),
            P(("grp", "sec"), None, None),
            P(("grp", "sec"), None, None),
            P(("grp", "sec")),
            P(("grp", "sec")),
            P(("grp", "sec")),
        ),
        out_specs=P("grp", "sec", None),
        check_vma=False,
    )
```

time: 429 us -> 71.5 us (0.17)
  the two profiles are of different devices: /device:TPU:256 before, /device:TPU:8 now
where the time goes in v1:
time: 71.5 us; the launch traced here: 71.2 us
  Pallas kernels  67.5 us (94%)
  local copies, waits for them, and re-layouts  3 us (4%)
    pallas_call x1, Pallas kernels, on_device(): pl.pallas_call(kernel, out_shape=jax.ShapeDtypeStruct((sectors, block, or...  67.5 us
    transpose x1, local copies, waits for them, and re-layouts, on_device(): return result.transpose(1, 0, 2)  1.52 us
    unnamed x1, local copies, waits for them, and re-layouts  1.48 us

profile of v1, /device:TPU:8, one launch (start us, length us, event | category | flops | bytes accessed | tf_op | source)
XLA Modules:
  0.0 71.2 jit_solution(17765610663276639753)
XLA Ops:
  0.7 1.5 %copy.10 = bf16[16,4,512]{2,0,1:T(8,128)(2,1)} copy(bf16[16,4,512]{2,1,0:T(4,128)(2,1)} %param.6) | data formatting | bytes 131072 | tf_op args[0]
  2.1 67.5 %gather_apply_scatter.1 = bf16[4,16,512]{2,1,0:T(8,128)(2,1)} custom-call(s32[4]{0:T(128)} %in_ref.1, s32[4]{0:T(128)} %out_ref.1, s32[1]{0:T(128)S(6)} %copy.11.count_ref, bf16[4,16,512]{2,1,0:T(8,128)(2,1)} %bitcast.5, bf16[4,512,512]{2,1,0:T(8,128)(2,1)} %left_hbm.1, bf16[4,512,512]{2,1,0:T(8,128)(2,1)} %right_hbm.1), custom_call_target="tpu_custom_call" | custom-call | tf_op jit(solution)/shard_map/gather_apply_scatter/pallas_call | solution.py:185
  69.6 1.5 %copy.8 = bf16[16,4,512]{2,1,0:T(4,128)(2,1)} copy(bf16[16,4,512]{2,0,1:T(8,128)(2,1)} %bitcast.4) | data formatting | bytes 131072 | tf_op jit(solution)/shard_map/transpose | solution.py:210

commit v2 on v1

v2 whole, which is shorter than its diff:
```python
import jax
import jax.numpy as jnp
from jax import lax
from jax.experimental import pallas as pl
from jax.experimental.pallas import tpu as pltpu
from jax.sharding import PartitionSpec as P

NX, NY = 4, 8
MESH = pl.DeviceIdType.MESH


def kernel(
    in_ref, out_ref, count_ref, own_ref, left_hbm, right_hbm, o_ref,
    state0, state1, left, right, prod, part, fbuf, gbuf,
    y_send, y_recv, x_send, x_recv, v_send, v_recv, u_send, u_recv,
    load_sem, agx_ss, agx_rs, agy_ss, agy_rs, agv_ss, agv_rs, agu_ss, agu_rs,
    rsy_ss, rsy_rs, rsx_ss, rsx_rs, rsv_ss, rsv_rs, rsu_ss, rsu_rs,
):
    g = lax.axis_index("grp")
    x, y = g // NY, lax.rem(g, NY)
    half = o_ref.shape[2] // 2

    def dev(dx, dy):
        return {"grp": lax.rem(x + dx + NX, NX) * NY + lax.rem(y + dy + NY, NY)}

    loads = [
        pltpu.make_async_copy(left_hbm, left, load_sem.at[0]),
        pltpu.make_async_copy(right_hbm, right, load_sem.at[1]),
        pltpu.make_async_copy(own_ref.at[0], state0.at[x, y], load_sem.at[2]),
        pltpu.make_async_copy(own_ref.at[1], state1.at[x, y], load_sem.at[3]),
    ]
    for load in loads:
        load.start()

    barrier = pltpu.get_barrier_semaphore()
    peers = [(1, 0), (2, 0), (3, 0), (0, 1), (0, -1)]
    for dx, dy in peers:
        pl.semaphore_signal(barrier, inc=1, device_id=dev(dx, dy), device_id_type=MESH)
    pl.semaphore_wait(barrier, len(peers))

    started = []

    def remote(src, dst, ss, rs, where):
        copy = pltpu.make_async_remote_copy(
            src_ref=src, dst_ref=dst, send_sem=ss, recv_sem=rs, device_id=where, device_id_type=MESH
        )
        copy.start()
        started.append(copy)
        return copy

    def ring(k, h, d):
        block = lax.rem(y - d * (k - 1) + NY, NY)
        piece = state0.at[2 * h:2 * h + 2, block]
        i = (1 - d) // 2
        return remote(piece, piece, agy_ss.at[i, k - 1, h], agy_rs.at[i, k - 1, h], dev(0, d))

    held = {}

    def ring_round(k):
        for h in range(2):
            for d in (1, -1):
                if k > 1:
                    held[k - 1, h, d].wait_recv()
                if k < 4 or (h == 0) == (d == 1):
                    held[k, h, d] = ring(k, h, d)

    passed, crossed, forwarded = {}, {}, {}
    blocks = [(0, 1), (1, 1), (1, -1), (2, 1), (2, -1), (3, 1), (3, -1), (4, 1)]

    def pass_on(k, d):
        i = (1 - d) // 2
        here = own_ref.at[1] if k == 1 else state1.at[x, lax.rem(y - d * (k - 1) + NY, NY)]
        there = state1.at[x, lax.rem(y - d * (k - 1) + NY, NY)]
        if k == 4:
            here, there = here.at[2 * i:2 * i + 2], there.at[2 * i:2 * i + 2]
        passed[k, d] = remote(here, there, agv_ss.at[i, k - 1], agv_rs.at[i, k - 1], dev(0, d))

    def cross(k, d):
        p = blocks.index((k, d))
        there = state1.at[x, lax.rem(y - d * k + NY, NY)]
        here = own_ref.at[1] if k == 0 else there
        for i in range(2):
            crossed[k, d, i] = remote(here, there, agu_ss.at[p, i], agu_rs.at[p, i], dev(1 - 2 * i, 0))

    def forward(k, d):
        p = blocks.index((k, d))
        way = {0: 1, 1: d, 2: -d, 3: d, 4: -1}[k]
        crossed[k, d, (1 - way) // 2].wait_recv()
        piece = state1.at[lax.rem(x - way + NX, NX), lax.rem(y - d * k + NY, NY)]
        forwarded[k, d] = remote(piece, piece, agu_ss.at[p, 2], agu_rs.at[p, 2], dev(way, 0))
        return crossed[k, d, (1 + way) // 2]

    gx = [
        remote(own_ref.at[0], state0.at[x, y], agx_ss.at[j - 1], agx_rs.at[j - 1], dev(j, 0))
        for j in (1, 3, 2)
    ]
    pass_on(1, 1), pass_on(1, -1), cross(0, 1)
    loads[2].wait()
    loads[3].wait()
    for copy in gx:
        copy.wait_recv()
    ring_round(1)
    rest = []
    before = [(0, 1)]
    for k in range(1, 5):
        for d in (1, -1):
            passed[k, d].wait_recv()
        for d in (1, -1):
            if k < 4:
                pass_on(k + 1, d)
        now = [(k, 1), (k, -1)] if k < 4 else [(4, 1)]
        for which in now:
            cross(*which)
        for which in before:
            rest.append(forward(*which))
        before = now
        if k < 4:
            ring_round(k + 1)
    held[4, 0, 1].wait_recv()
    held[4, 1, -1].wait_recv()

    loads[0].wait()
    rows = NX * NY * own_ref.shape[2]

    def first(q, c):
        block = (state0, state1)[c][:, :, in_ref[q]].reshape(rows, half)
        prod[q, :, c * half:(c + 1) * half] = jnp.dot(
            left[q], block, preferred_element_type=jnp.float32
        ).astype(jnp.bfloat16)

    first(0, 0)
    rest.append(forward(4, 1))
    for q in range(1, 4):
        first(q, 0)
    for copy in rest:
        copy.wait_recv()
    for copy in forwarded.values():
        copy.wait_recv()
    for q in range(4):
        first(q, 1)
    loads[1].wait()

    weight = [
        [
            jnp.where((out_ref[q] == t) & (q < count_ref[0]), jnp.float32(1), jnp.float32(0))
            for t in range(4)
        ]
        for q in range(4)
    ]

    def second(c, h):
        span = slice(h * (rows // 2), (h + 1) * (rows // 2))
        proj = [
            lax.dot_general(
                prod[q, span], right[q, c * half:(c + 1) * half],
                (((1,), (1,)), ((), ())), preferred_element_type=jnp.float32,
            )
            for q in range(4)
        ]
        for t in range(4):
            total = proj[0] * weight[0][t]
            for q in range(1, 4):
                total = total + proj[q] * weight[q][t]
            part[c, 2 * h:2 * h + 2, :, t] = total.reshape(2, NY, own_ref.shape[2], half)

    def scatter_y_x(c):
        got = {}

        def step(k, h, d):
            i = (1 - d) // 2
            value = part[c, 2 * h:2 * h + 2, lax.rem(y + d * k + NY, NY)]
            if (k + 1, h, d) in got:
                got[k + 1, h, d].wait_recv()
                value = value + y_recv[i, k, h].astype(jnp.float32)
            y_send[i, k - 1, h] = value.astype(jnp.bfloat16)
            got[k, h, d] = remote(
                y_send.at[i, k - 1, h], y_recv.at[i, k - 1, h],
                rsy_ss.at[i, k - 1, h], rsy_rs.at[i, k - 1, h], dev(0, d),
            )

        step(4, 0, 1), step(4, 1, -1), step(3, 1, 1), step(3, 0, -1)
        yield
        step(3, 0, 1), step(3, 1, -1)
        yield
        for k in (2, 1):
            step(k, 1, 1), step(k, 0, -1)
            yield
            step(k, 0, 1), step(k, 1, -1)
            yield
        for h in (0, 1):
            value = part[c, 2 * h:2 * h + 2, y]
            for d in (1, -1):
                got[1, h, d].wait_recv()
                value = value + y_recv[(1 - d) // 2, 0, h].astype(jnp.float32)
            fbuf[2 * h:2 * h + 2] = value
        cross = []
        for j in (2, 1, 3):
            x_send[j - 1] = fbuf[lax.rem(x + j, NX)].astype(jnp.bfloat16)
            cross.append(remote(
                x_send.at[j - 1], x_recv.at[j - 1],
                rsx_ss.at[j - 1], rsx_rs.at[j - 1], dev(j, 0),
            ))
        yield
        value = fbuf[x]
        for copy in cross:
            copy.wait_recv()
        for j in (1, 2, 3):
            value = value + x_recv[j - 1].astype(jnp.float32)
        o_ref[:, :, c * half:(c + 1) * half] = value.astype(jnp.bfloat16)

    groups = [(4, 3), (-3, 2), (-2, 1), (-1, 0)]

    def scatter_x_y(c):
        got = {}

        def block(dx, j):
            return part[c, lax.rem(x + dx + NX, NX), lax.rem(y + j + NY, NY)]

        def step(n, k, d):
            main = 1 - 2 * (n % 2)
            kind = 0 if k == 2 else (1 if d == main else 2)
            for m, j in enumerate(groups[n]):
                value = block(d * k, j)
                if kind == 1:
                    if m == 0:
                        got[n, 0].wait_recv()
                    value = value + u_recv[0, n, m].astype(jnp.float32)
                u_send[kind, n, m] = value.astype(jnp.bfloat16)
            got[n, kind] = remote(
                u_send.at[kind, n], u_recv.at[kind, n], rsu_ss.at[kind, n], rsu_rs.at[kind, n], dev(d, 0)
            )

        def settle(n):
            got[n, 1].wait_recv()
            got[n, 2].wait_recv()
            for m, j in enumerate(groups[n]):
                gbuf[j + 3] = (
                    block(0, j) + u_recv[1, n, m].astype(jnp.float32) + u_recv[2, n, m].astype(jnp.float32)
                )

        def pass_back(k, d):
            i = (1 - d) // 2
            value = gbuf[d * k + 3]
            if (d, k + 1) in got:
                got[d, k + 1].wait_recv()
                value = value + v_recv[i, k].astype(jnp.float32)
            v_send[i, k - 1] = value.astype(jnp.bfloat16)
            got[d, k] = remote(
                v_send.at[i, k - 1], v_recv.at[i, k - 1], rsv_ss.at[i, k - 1], rsv_rs.at[i, k - 1], dev(0, d)
            )

        step(0, 2, 1), step(1, 2, -1), step(2, 2, 1), step(3, 2, -1)
        step(0, 1, -1), step(1, 1, 1)
        yield
        step(0, 1, 1), step(1, 1, -1)
        step(2, 1, -1), step(3, 1, 1)
        yield
        step(2, 1, 1), step(3, 1, -1)
        yield
        settle(0)
        pass_back(4, 1)
        settle(1)
        pass_back(3, -1)
        yield
        settle(2)
        pass_back(3, 1), pass_back(2, -1)
        yield
        settle(3)
        pass_back(2, 1), pass_back(1, -1)
        yield
        pass_back(1, 1)
        yield
        value = gbuf[3]
        for i, d in ((0, 1), (1, -1)):
            got[d, 1].wait_recv()
            value = value + v_recv[i, 0].astype(jnp.float32)
        o_ref[:, :, c * half:(c + 1) * half] = value.astype(jnp.bfloat16)

    second(1, 0)
    second(1, 1)
    flow0, flow1 = scatter_y_x(0), scatter_x_y(1)
    next(flow1)
    second(0, 0)
    next(flow1)
    second(0, 1)
    next(flow0)
    live = [flow1, flow0]
    while live:
        for flow in list(live):
            try:
                next(flow)
            except StopIteration:
                live.remove(flow)
    for copy in started:
        copy.wait_send()


def on_device(wavefunction, left_ops, right_ops, in_sector, out_sector, term_count):
    block, sectors, order = wavefunction.shape
    half = order // 2
    own = wavefunction.reshape(block, sectors, 2, half).transpose(2, 1, 0, 3)
    slots = left_ops.shape[0]
    piece = (sectors, block, half)
    vmem = pl.BlockSpec(memory_space=pltpu.VMEM)
    smem = pl.BlockSpec(memory_space=pltpu.SMEM)
    hbm = pl.BlockSpec(memory_space=pl.ANY)
    dma = pltpu.SemaphoreType.DMA
    result = pl.pallas_call(
        kernel,
        out_shape=jax.ShapeDtypeStruct((sectors, block, order), jnp.bfloat16),
        in_specs=[smem, smem, smem, vmem, hbm, hbm],
        out_specs=vmem,
        scratch_shapes=[
            pltpu.VMEM((NX, NY, *piece), jnp.bfloat16),
            pltpu.VMEM((NX, NY, *piece), jnp.bfloat16),
            pltpu.VMEM(left_ops.shape, jnp.bfloat16),
            pltpu.VMEM(right_ops.shape, jnp.bfloat16),
            pltpu.VMEM((slots, left_ops.shape[1], order), jnp.bfloat16),
            pltpu.VMEM((2, NX, NY, *piece), jnp.float32),
            pltpu.VMEM((NX, *piece), jnp.float32),
            pltpu.VMEM((NY, *piece), jnp.float32),
            pltpu.VMEM((2, 4, 2, 2, *piece), jnp.bfloat16),
            pltpu.VMEM((2, 4, 2, 2, *piece), jnp.bfloat16),
            pltpu.VMEM((3, *piece), jnp.bfloat16),
            pltpu.VMEM((3, *piece), jnp.bfloat16),
            pltpu.VMEM((2, 4, *piece), jnp.bfloat16),
            pltpu.VMEM((2, 4, *piece), jnp.bfloat16),
            pltpu.VMEM((3, 4, 2, *piece), jnp.bfloat16),
            pltpu.VMEM((3, 4, 2, *piece), jnp.bfloat16),
            dma((4,)),
            dma((3,)), dma((3,)),
            dma((2, 4, 2)), dma((2, 4, 2)),
            dma((2, 4)), dma((2, 4)),
            dma((8, 3)), dma((8, 3)),
            dma((2, 4, 2)), dma((2, 4, 2)),
            dma((3,)), dma((3,)),
            dma((2, 4)), dma((2, 4)),
            dma((3, 4)), dma((3, 4)),
        ],
        compiler_params=pltpu.CompilerParams(collective_id=0, has_side_effects=True),
        name="gather_apply_scatter",
    )(in_sector, out_sector, term_count, own, left_ops, right_ops)
    return result.transpose(1, 0, 2)


def solution(mesh):
    return jax.shard_map(
        on_device,
        mesh=mesh,
        in_specs=(
            P("grp", "sec", None),
            P(("grp", "sec"), None, None),
            P(("grp", "sec"), None, None),
            P(("grp", "sec")),
            P(("grp", "sec")),
            P(("grp", "sec")),
        ),
        out_specs=P("grp", "sec", None),
        check_vma=False,
    )
```

time: 71.5 us -> 68.5 us (0.958)
  Pallas kernels: 67.5 us -> 64.5 us
    pallas_call x1, Pallas kernels: 67.5 us -> 64.5 us  [on_device(): pl.pallas_call(kernel, out_shape=jax.ShapeDtypeStruct((sectors, block, or...]
    reshape x0 -> x2, local copies, waits for them, and re-layouts: none -> 1.52 us  [on_device(): own = wavefunction.reshape(block, sectors, 2, half).transpose(2, 1, 0, 3)]
    unnamed x1 -> x0, local copies, waits for them, and re-layouts: 1.48 us -> none
where the time goes in v2:
time: 68.5 us; the launch traced here: 68.2 us
  Pallas kernels  64.5 us (94%)
  local copies, waits for them, and re-layouts  3.04 us (4%)
    pallas_call x1, Pallas kernels, on_device(): pl.pallas_call(kernel, out_shape=jax.ShapeDtypeStruct((sectors, block, or...  64.5 us
    transpose x1, local copies, waits for them, and re-layouts, on_device(): return result.transpose(1, 0, 2)  1.52 us
    reshape x2, local copies, waits for them, and re-layouts, on_device(): own = wavefunction.reshape(block, sectors, 2, half).transpose(2, 1, 0, 3)  1.52 us

profile of v2, /device:TPU:8, one launch (start us, length us, event | category | flops | bytes accessed | tf_op | source)
XLA Modules:
  0.0 68.2 jit_solution(5803212798280306849)
XLA Ops:
  0.7 0.9 %reshape.4 = bf16[16,4,2,256]{3,2,1,0:T(2,128)(2,1)S(1)} reshape(bf16[16,4,512]{2,1,0:T(4,128)(2,1)} %param.6) | data formatting | bytes 131072 | tf_op jit(solution)/shard_map/reshape | solution.py:301
  1.5 0.6 copy.14
  2.2 64.5 %gather_apply_scatter.1 = bf16[4,16,512]{2,1,0:T(8,128)(2,1)} custom-call(s32[4]{0:T(128)} %in_ref.1, s32[4]{0:T(128)} %out_ref.1, s32[1]{0:T(128)S(6)} %copy.15.count_ref, bf16[2,4,16,256]{3,2,1,0:T(8,128)(2,1)} %bitcast.4, bf16[4,512,512]{2,1,0:T(8,128)(2,1)} %left_hbm.1, bf16[4,512,512]{2,1,0:T(8,128)(2,1)} %right_hbm.1), custom_call_target="tpu_custom_call" | custom-call | tf_op jit(solution)/shard_map/gather_apply_scatter/pallas_call | solution.py:308
  66.7 1.5 %copy.10 = bf16[16,4,512]{2,1,0:T(4,128)(2,1)} copy(bf16[16,4,512]{2,0,1:T(8,128)(2,1)} %bitcast.5) | data formatting | bytes 131072 | tf_op jit(solution)/shard_map/transpose | solution.py:343

commit v3 on v2

--- a/solution.py
+++ b/solution.py
@@ -33,7 +33,7 @@
         load.start()
 
     barrier = pltpu.get_barrier_semaphore()
-    peers = [(1, 0), (2, 0), (3, 0), (0, 1), (0, -1)]
+    peers = [(j, 0) for j in range(1, NX)] + [(0, j) for j in range(1, NY)]
     for dx, dy in peers:
         pl.semaphore_signal(barrier, inc=1, device_id=dev(dx, dy), device_id_type=MESH)
     pl.semaphore_wait(barrier, len(peers))
@@ -64,58 +64,40 @@
                 if k < 4 or (h == 0) == (d == 1):
                     held[k, h, d] = ring(k, h, d)
 
-    passed, crossed, forwarded = {}, {}, {}
-    blocks = [(0, 1), (1, 1), (1, -1), (2, 1), (2, -1), (3, 1), (3, -1), (4, 1)]
-
-    def pass_on(k, d):
-        i = (1 - d) // 2
-        here = own_ref.at[1] if k == 1 else state1.at[x, lax.rem(y - d * (k - 1) + NY, NY)]
-        there = state1.at[x, lax.rem(y - d * (k - 1) + NY, NY)]
-        if k == 4:
-            here, there = here.at[2 * i:2 * i + 2], there.at[2 * i:2 * i + 2]
-        passed[k, d] = remote(here, there, agv_ss.at[i, k - 1], agv_rs.at[i, k - 1], dev(0, d))
-
-    def cross(k, d):
-        p = blocks.index((k, d))
-        there = state1.at[x, lax.rem(y - d * k + NY, NY)]
-        here = own_ref.at[1] if k == 0 else there
-        for i in range(2):
-            crossed[k, d, i] = remote(here, there, agu_ss.at[p, i], agu_rs.at[p, i], dev(1 - 2 * i, 0))
-
-    def forward(k, d):
-        p = blocks.index((k, d))
-        way = {0: 1, 1: d, 2: -d, 3: d, 4: -1}[k]
-        crossed[k, d, (1 - way) // 2].wait_recv()
-        piece = state1.at[lax.rem(x - way + NX, NX), lax.rem(y - d * k + NY, NY)]
-        forwarded[k, d] = remote(piece, piece, agu_ss.at[p, 2], agu_rs.at[p, 2], dev(way, 0))
-        return crossed[k, d, (1 + way) // 2]
+    passed, crossed = {}, []
+
+    def pass_on(j):
+        passed[j] = remote(
+            own_ref.at[1], state1.at[x, y], agv_ss.at[j + 3], agv_rs.at[j + 3], dev(0, j)
+        )
+
+    def cross(j):
+        there = state1.at[x, lax.rem(y - j + NY, NY)]
+        if j:
+            passed[j].wait_recv()
+        for i in (1, 3, 2):
+            crossed.append(remote(
+                there if j else own_ref.at[1], there, agu_ss.at[j + 3, i - 1], agu_rs.at[j + 3, i - 1], dev(i, 0)
+            ))
 
     gx = [
         remote(own_ref.at[0], state0.at[x, y], agx_ss.at[j - 1], agx_rs.at[j - 1], dev(j, 0))
         for j in (1, 3, 2)
     ]
-    pass_on(1, 1), pass_on(1, -1), cross(0, 1)
+    for j in (1, -1, 2, -2, 3, -3, 4):
+        pass_on(j)
+    cross(0)
     loads[2].wait()
-    loads[3].wait()
     for copy in gx:
         copy.wait_recv()
     ring_round(1)
-    rest = []
-    before = [(0, 1)]
-    for k in range(1, 5):
-        for d in (1, -1):
-            passed[k, d].wait_recv()
-        for d in (1, -1):
-            if k < 4:
-                pass_on(k + 1, d)
-        now = [(k, 1), (k, -1)] if k < 4 else [(4, 1)]
-        for which in now:
-            cross(*which)
-        for which in before:
-            rest.append(forward(*which))
-        before = now
-        if k < 4:
-            ring_round(k + 1)
+    cross(1), cross(-1)
+    ring_round(2)
+    cross(2), cross(-2), cross(3), cross(-3)
+    ring_round(3)
+    cross(4)
+    ring_round(4)
+    loads[3].wait()
     held[4, 0, 1].wait_recv()
     held[4, 1, -1].wait_recv()
 
@@ -128,13 +110,9 @@
             left[q], block, preferred_element_type=jnp.float32
         ).astype(jnp.bfloat16)
 
-    first(0, 0)
-    rest.append(forward(4, 1))
-    for q in range(1, 4):
+    for q in range(4):
         first(q, 0)
-    for copy in rest:
-        copy.wait_recv()
-    for copy in forwarded.values():
+    for copy in crossed:
         copy.wait_recv()
     for q in range(4):
         first(q, 1)
@@ -211,69 +189,44 @@
     groups = [(4, 3), (-3, 2), (-2, 1), (-1, 0)]
 
     def scatter_x_y(c):
-        got = {}
+        got, last = {}, []
 
         def block(dx, j):
-            return part[c, lax.rem(x + dx + NX, NX), lax.rem(y + j + NY, NY)]
-
-        def step(n, k, d):
-            main = 1 - 2 * (n % 2)
-            kind = 0 if k == 2 else (1 if d == main else 2)
+            return part[c, lax.rem(x + dx, NX), lax.rem(y + j + NY, NY)]
+
+        def spread(n):
+            for i in (2, 1, 3):
+                for m, j in enumerate(groups[n]):
+                    u_send[n, i - 1, m] = block(i, j).astype(jnp.bfloat16)
+                got[n, i] = remote(
+                    u_send.at[n, i - 1], u_recv.at[n, i - 1],
+                    rsu_ss.at[n, i - 1], rsu_rs.at[n, i - 1], dev(i, 0),
+                )
+
+        def settle(n):
+            for i in (1, 3, 2):
+                got[n, i].wait_recv()
             for m, j in enumerate(groups[n]):
-                value = block(d * k, j)
-                if kind == 1:
-                    if m == 0:
-                        got[n, 0].wait_recv()
-                    value = value + u_recv[0, n, m].astype(jnp.float32)
-                u_send[kind, n, m] = value.astype(jnp.bfloat16)
-            got[n, kind] = remote(
-                u_send.at[kind, n], u_recv.at[kind, n], rsu_ss.at[kind, n], rsu_rs.at[kind, n], dev(d, 0)
-            )
-
-        def settle(n):
-            got[n, 1].wait_recv()
-            got[n, 2].wait_recv()
-            for m, j in enumerate(groups[n]):
-                gbuf[j + 3] = (
-                    block(0, j) + u_recv[1, n, m].astype(jnp.float32) + u_recv[2, n, m].astype(jnp.float32)
-                )
-
-        def pass_back(k, d):
-            i = (1 - d) // 2
-            value = gbuf[d * k + 3]
-            if (d, k + 1) in got:
-                got[d, k + 1].wait_recv()
-                value = value + v_recv[i, k].astype(jnp.float32)
-            v_send[i, k - 1] = value.astype(jnp.bfloat16)
-            got[d, k] = remote(
-                v_send.at[i, k - 1], v_recv.at[i, k - 1], rsv_ss.at[i, k - 1], rsv_rs.at[i, k - 1], dev(0, d)
-            )
-
-        step(0, 2, 1), step(1, 2, -1), step(2, 2, 1), step(3, 2, -1)
-        step(0, 1, -1), step(1, 1, 1)
+                value = block(0, j)
+                for i in range(3):
+                    value = value + u_recv[n, i, m].astype(jnp.float32)
+                if j == 0:
+                    gbuf[...] = value
+                else:
+                    v_send[j + 3] = value.astype(jnp.bfloat16)
+                    last.append((j + 3, remote(
+                        v_send.at[j + 3], v_recv.at[j + 3], rsv_ss.at[j + 3], rsv_rs.at[j + 3], dev(0, j)
+                    )))
+
+        spread(0), spread(1), spread(2), spread(3)
         yield
-        step(0, 1, 1), step(1, 1, -1)
-        step(2, 1, -1), step(3, 1, 1)
-        yield
-        step(2, 1, 1), step(3, 1, -1)
-        yield
-        settle(0)
-        pass_back(4, 1)
-        settle(1)
-        pass_back(3, -1)
-        yield
-        settle(2)
-        pass_back(3, 1), pass_back(2, -1)
-        yield
-        settle(3)
-        pass_back(2, 1), pass_back(1, -1)
-        yield
-        pass_back(1, 1)
-        yield
-        value = gbuf[3]
-        for i, d in ((0, 1), (1, -1)):
-            got[d, 1].wait_recv()
-            value = value + v_recv[i, 0].astype(jnp.float32)
+        for n in range(4):
+            settle(n)
+            yield
+        value = gbuf[...]
+        for slot, copy in last:
+            copy.wait_recv()
+            value = value + v_recv[slot].astype(jnp.float32)
         o_ref[:, :, c * half:(c + 1) * half] = value.astype(jnp.bfloat16)
 
     second(1, 0)
@@ -281,10 +234,9 @@
     flow0, flow1 = scatter_y_x(0), scatter_x_y(1)
     next(flow1)
     second(0, 0)
-    next(flow1)
     second(0, 1)
     next(flow0)
-    live = [flow1, flow0]
+    live = [flow0, flow1]
     while live:
         for flow in list(live):
             try:
@@ -318,24 +270,24 @@
             pltpu.VMEM((slots, left_ops.shape[1], order), jnp.bfloat16),
             pltpu.VMEM((2, NX, NY, *piece), jnp.float32),
             pltpu.VMEM((NX, *piece), jnp.float32),
-            pltpu.VMEM((NY, *piece), jnp.float32),
+            pltpu.VMEM(piece, jnp.float32),
             pltpu.VMEM((2, 4, 2, 2, *piece), jnp.bfloat16),
             pltpu.VMEM((2, 4, 2, 2, *piece), jnp.bfloat16),
             pltpu.VMEM((3, *piece), jnp.bfloat16),
             pltpu.VMEM((3, *piece), jnp.bfloat16),
-            pltpu.VMEM((2, 4, *piece), jnp.bfloat16),
-            pltpu.VMEM((2, 4, *piece), jnp.bfloat16),
-            pltpu.VMEM((3, 4, 2, *piece), jnp.bfloat16),
-            pltpu.VMEM((3, 4, 2, *piece), jnp.bfloat16),
+            pltpu.VMEM((8, *piece), jnp.bfloat16),
+            pltpu.VMEM((8, *piece), jnp.bfloat16),
+            pltpu.VMEM((4, 3, 2, *piece), jnp.bfloat16),
+            pltpu.VMEM((4, 3, 2, *piece), jnp.bfloat16),
             dma((4,)),
             dma((3,)), dma((3,)),
             dma((2, 4, 2)), dma((2, 4, 2)),
-            dma((2, 4)), dma((2, 4)),
+            dma((8,)), dma((8,)),
             dma((8, 3)), dma((8, 3)),
             dma((2, 4, 2)), dma((2, 4, 2)),
             dma((3,)), dma((3,)),
-            dma((2, 4)), dma((2, 4)),
-            dma((3, 4)), dma((3, 4)),
+            dma((8,)), dma((8,)),
+            dma((4, 3)), dma((4, 3)),
         ],
         compiler_params=pltpu.CompilerParams(collective_id=0, has_side_effects=True),
         name="gather_apply_scatter",

time: 68.5 us -> 61.8 us (0.902)
  Pallas kernels: 64.5 us -> 57.9 us
    pallas_call x1, Pallas kernels: 64.5 us -> 57.9 us  [on_device(): pl.pallas_call(kernel, out_shape=jax.ShapeDtypeStruct((sectors, block, or...]
where the time goes in v3:
time: 61.8 us; the launch traced here: 61.6 us
  Pallas kernels  57.9 us (94%)
  local copies, waits for them, and re-layouts  3.04 us (5%)
  between operations  0.66 us (1%)
    pallas_call x1, Pallas kernels, on_device(): pl.pallas_call(kernel, out_shape=jax.ShapeDtypeStruct((sectors, block, or...  57.9 us
    transpose x1, local copies, waits for them, and re-layouts, on_device(): return result.transpose(1, 0, 2)  1.52 us
    reshape x2, local copies, waits for them, and re-layouts, on_device(): own = wavefunction.reshape(block, sectors, 2, half).transpose(2, 1, 0, 3)  1.52 us

profile of v3, /device:TPU:8, one launch (start us, length us, event | category | flops | bytes accessed | tf_op | source)
XLA Modules:
  0.0 61.6 jit_solution(6403715188597636233)
XLA Ops:
  0.7 0.9 %reshape.4 = bf16[16,4,2,256]{3,2,1,0:T(2,128)(2,1)S(1)} reshape(bf16[16,4,512]{2,1,0:T(4,128)(2,1)} %param.6) | data formatting | bytes 131072 | tf_op jit(solution)/shard_map/reshape | solution.py:253
  1.5 0.6 %copy.14 = bf16[16,4,2,256]{3,0,1,2:T(8,128)(2,1)} copy(bf16[16,4,2,256]{3,2,1,0:T(2,128)(2,1)S(1)} %reshape.4) | data formatting | bytes 131072 | tf_op jit(solution)/shard_map/reshape | solution.py:253
  2.2 57.9 %gather_apply_scatter.1 = bf16[4,16,512]{2,1,0:T(8,128)(2,1)} custom-call(s32[4]{0:T(128)} %in_ref.1, s32[4]{0:T(128)} %out_ref.1, s32[1]{0:T(128)S(6)} %copy.15.count_ref, bf16[2,4,16,256]{3,2,1,0:T(8,128)(2,1)} %bitcast.4, bf16[4,512,512]{2,1,0:T(8,128)(2,1)} %left_hbm.1, bf16[4,512,512]{2,1,0:T(8,128)(2,1)} %right_hbm.1), custom_call_target="tpu_custom_call" | custom-call | tf_op jit(solution)/shard_map/gather_apply_scatter/pallas_call | solution.py:260
  60.0 1.5 %copy.10 = bf16[16,4,512]{2,1,0:T(4,128)(2,1)} copy(bf16[16,4,512]{2,0,1:T(8,128)(2,1)} %bitcast.5) | data formatting | bytes 131072 | tf_op jit(solution)/shard_map/transpose | solution.py:295

commit v4 on v3

--- a/solution.py
+++ b/solution.py
@@ -10,8 +10,8 @@
 
 
 def kernel(
-    in_ref, out_ref, count_ref, own_ref, left_hbm, right_hbm, o_ref,
-    state0, state1, left, right, prod, part, fbuf, gbuf,
+    in_ref, out_ref, count_ref, wave_ref, left_hbm, right_hbm, o_ref,
+    own_ref, state0, state1, left, right, prod, part, fbuf, gbuf,
     y_send, y_recv, x_send, x_recv, v_send, v_recv, u_send, u_recv,
     load_sem, agx_ss, agx_rs, agy_ss, agy_rs, agv_ss, agv_rs, agu_ss, agu_rs,
     rsy_ss, rsy_rs, rsx_ss, rsx_rs, rsv_ss, rsv_rs, rsu_ss, rsu_rs,
@@ -22,6 +22,11 @@
 
     def dev(dx, dy):
         return {"grp": lax.rem(x + dx + NX, NX) * NY + lax.rem(y + dy + NY, NY)}
+
+    block = wave_ref[...].astype(jnp.float32)
+    for s in range(block.shape[1]):
+        for c in range(2):
+            own_ref[c, s] = block[:, s, c * half:(c + 1) * half].astype(jnp.bfloat16)
 
     loads = [
         pltpu.make_async_copy(left_hbm, left, load_sem.at[0]),
@@ -38,7 +43,7 @@
         pl.semaphore_signal(barrier, inc=1, device_id=dev(dx, dy), device_id_type=MESH)
     pl.semaphore_wait(barrier, len(peers))
 
-    started = []
+    started, done = [], {}
 
     def remote(src, dst, ss, rs, where):
         copy = pltpu.make_async_remote_copy(
@@ -184,7 +189,7 @@
             copy.wait_recv()
         for j in (1, 2, 3):
             value = value + x_recv[j - 1].astype(jnp.float32)
-        o_ref[:, :, c * half:(c + 1) * half] = value.astype(jnp.bfloat16)
+        done[c] = value
 
     groups = [(4, 3), (-3, 2), (-2, 1), (-1, 0)]
 
@@ -227,7 +232,7 @@
         for slot, copy in last:
             copy.wait_recv()
             value = value + v_recv[slot].astype(jnp.float32)
-        o_ref[:, :, c * half:(c + 1) * half] = value.astype(jnp.bfloat16)
+        done[c] = value
 
     second(1, 0)
     second(1, 1)
@@ -243,6 +248,7 @@
                 next(flow)
             except StopIteration:
                 live.remove(flow)
+    o_ref[...] = jnp.swapaxes(jnp.concatenate([done[0], done[1]], axis=2), 0, 1).astype(jnp.bfloat16)
     for copy in started:
         copy.wait_send()
 
@@ -250,19 +256,19 @@
 def on_device(wavefunction, left_ops, right_ops, in_sector, out_sector, term_count):
     block, sectors, order = wavefunction.shape
     half = order // 2
-    own = wavefunction.reshape(block, sectors, 2, half).transpose(2, 1, 0, 3)
     slots = left_ops.shape[0]
     piece = (sectors, block, half)
     vmem = pl.BlockSpec(memory_space=pltpu.VMEM)
     smem = pl.BlockSpec(memory_space=pltpu.SMEM)
     hbm = pl.BlockSpec(memory_space=pl.ANY)
     dma = pltpu.SemaphoreType.DMA
-    result = pl.pallas_call(
+    return pl.pallas_call(
         kernel,
-        out_shape=jax.ShapeDtypeStruct((sectors, block, order), jnp.bfloat16),
+        out_shape=jax.ShapeDtypeStruct(wavefunction.shape, jnp.bfloat16),
         in_specs=[smem, smem, smem, vmem, hbm, hbm],
         out_specs=vmem,
         scratch_shapes=[
+            pltpu.VMEM((2, *piece), jnp.bfloat16),
             pltpu.VMEM((NX, NY, *piece), jnp.bfloat16),
             pltpu.VMEM((NX, NY, *piece), jnp.bfloat16),
             pltpu.VMEM(left_ops.shape, jnp.bfloat16),
@@ -291,8 +297,7 @@
         ],
         compiler_params=pltpu.CompilerParams(collective_id=0, has_side_effects=True),
         name="gather_apply_scatter",
-    )(in_sector, out_sector, term_count, own, left_ops, right_ops)
-    return result.transpose(1, 0, 2)
+    )(in_sector, out_sector, term_count, wavefunction, left_ops, right_ops)
 
 
 def solution(mesh):

time: 61.8 us -> 60.4 us (0.977)
  local copies, waits for them, and re-layouts: 3.04 us -> 1.49 us
    transpose x1 -> x0, local copies, waits for them, and re-layouts: 1.52 us -> none  [on_device(): return result.transpose(1, 0, 2)]
    reshape x2 -> x0, local copies, waits for them, and re-layouts: 1.52 us -> none  [on_device(): own = wavefunction.reshape(block, sectors, 2, half).transpose(2, 1, 0, 3)]
    unnamed x0 -> x1, local copies, waits for them, and re-layouts: none -> 1.49 us
where the time goes in v4:
time: 60.4 us; the launch traced here: 60.2 us
  Pallas kernels  58 us (96%)
  local copies, waits for them, and re-layouts  1.49 us (2%)
  between operations  0.66 us (1%)
    pallas_call x1, Pallas kernels, on_device(): pl.pallas_call(kernel, out_shape=jax.ShapeDtypeStruct(wavefunction.shape,...  58 us
    unnamed x1, local copies, waits for them, and re-layouts  1.49 us

profile of v4, /device:TPU:8, one launch (start us, length us, event | category | flops | bytes accessed | tf_op | source)
XLA Modules:
  0.0 60.2 jit_solution(7414617016788944300)
XLA Ops:
  0.7 58.0 %gather_apply_scatter.1 = bf16[16,4,512]{2,1,0:T(4,128)(2,1)} custom-call(s32[4]{0:T(128)} %in_ref.1, s32[4]{0:T(128)} %out_ref.1, s32[1]{0:T(128)S(6)} %copy.8.count_ref, bf16[16,4,512]{2,1,0:T(4,128)(2,1)} %wave_ref.1, bf16[4,512,512]{2,1,0:T(8,128)(2,1)} %left_hbm.1, bf16[4,512,512]{2,1,0:T(8,128)(2,1)} %right_hbm.1), custom_call_target="tpu_custom_call" | custom-call | tf_op jit(solution)/shard_map/gather_apply_scatter/pallas_call | solution.py:265
  58.7 1.5 %copy.9 = bf16[16,4,512]{2,1,0:T(4,128)(2,1)} copy(bf16[16,4,512]{2,1,0:T(4,128)(2,1)} %gather_apply_scatter.1) | data formatting | bytes 131072
